TPU v7x, 512 devices: a whole 4x8x8 slice. The times are simulated.
512 devices in a mesh: dp: 16 (over y, core), seq: 32 (over x, z).
Axes of the slice: x: 4, y: 8, z: 8, core: 2. Of those that a mesh axis runs over, the one named last changes fastest.
Arguments:
- queries: bfloat16 [16, 4096, 2048], P('dp', 'seq'), may hold values from -40 to 40, as said below
- keys: bfloat16 [16, 4096, 2048], P('dp', 'seq'), may hold values from -40 to 40, as said below
- values: bfloat16 [16, 4096, 2048], P('dp', 'seq'), may hold values from -40 to 40, as said below
- gain: float32 [2048], replicated, may hold values from 0.1 to 1.9
- cotangent: bfloat16 [16, 4096, 2048], P('dp', 'seq'), may hold values from -240 to 240, as said below
Outputs:
- output: bfloat16 [16, 4096, 2048], P('dp', 'seq')
- grad_query: bfloat16 [16, 4096, 2048], P('dp', 'seq')
- grad_key: bfloat16 [16, 4096, 2048], P('dp', 'seq')
- grad_value: bfloat16 [16, 4096, 2048], P('dp', 'seq')
- gain_grad: float32 [2048], replicated
Inputs may be any that keep to these rules, and one draw needn't show every extreme that they name: queries: independent entries with row and feature scales. keys: independent entries with row and feature scales. values: independent entries with row and feature scales. cotangent: independent entries with row and feature scales.
All inputs are finite; a program needn't handle non-finite values.
Results may differ from a plain program's by a relative error of at most 0.0058.
Values may be sent and summed in bfloat16 or wider, within the bound.
A program may use at most 64 MiB of HBM per device.

v0:
```python
import jax
import jax.numpy as jnp
from jax import lax
from jax.sharding import PartitionSpec as P

HEADS = 16
EPSILON = 1e-06


def prefix_swapped(state_block, reverse_order):
    device_count = lax.axis_size("seq")
    flat_state = state_block.reshape(1, -1)
    columns = lax.all_to_all(flat_state, "seq", split_axis=1, concat_axis=0, tiled=True)
    device_rank = jnp.arange(device_count)
    if reverse_order:
        triangle = device_rank[None, :] > device_rank[:, None]
    else:
        triangle = device_rank[None, :] < device_rank[:, None]
    summed = jnp.dot(triangle.astype(jnp.float32), columns, precision=lax.Precision.HIGHEST)
    summed_half = summed.astype(jnp.bfloat16)
    returned = lax.all_to_all(summed_half, "seq", split_axis=0, concat_axis=1, tiled=True)
    return returned.reshape(state_block.shape)


def per_device(queries, keys, values, gain, cotangent):
    row_count = queries.shape[1]
    feature_count = queries.shape[2]
    head_size = feature_count // HEADS
    scaling = head_size ** (-0.5)
    query_rows = queries[0].reshape(row_count, HEADS, head_size)
    key_rows = keys[0].reshape(row_count, HEADS, head_size)
    value_rows = values[0].reshape(row_count, HEADS, head_size)
    kv_local = jnp.einsum("thd,the->hde", key_rows, value_rows, preferred_element_type=jnp.float32)
    prefix_half = prefix_swapped(kv_local, False)
    position = jnp.arange(row_count)
    causal_mask = (position[:, None] >= position[None, :]).astype(jnp.float32)
    scores = (
        jnp.einsum("thd,uhd->htu", query_rows, key_rows, preferred_element_type=jnp.float32)
        * scaling
        * causal_mask
    ).astype(jnp.bfloat16)
    attended = jnp.einsum("htu,uhe->the", scores, value_rows, preferred_element_type=jnp.float32)
    attended = attended + scaling * jnp.einsum(
        "thd,hde->the", query_rows, prefix_half, preferred_element_type=jnp.float32
    )
    attended = attended.reshape(row_count, feature_count)
    root_mean = jnp.sqrt(jnp.mean(attended * attended, axis=-1, keepdims=True) + EPSILON)
    normalized = attended / root_mean
    output = (gain * normalized).astype(jnp.bfloat16)[None]
    upstream = cotangent[0].astype(jnp.float32)
    partial_gain = jnp.sum(upstream * normalized, axis=0)
    total_gain = lax.psum(partial_gain, ("dp", "seq"))
    gain_grad = total_gain / lax.axis_size("dp")
    scaled = upstream * gain
    inner_mean = jnp.mean(scaled * normalized, axis=-1, keepdims=True)
    grad_attn = (
        ((scaled - normalized * inner_mean) / root_mean)
        .astype(jnp.bfloat16)
        .reshape(row_count, HEADS, head_size)
    )
    local_grads = scaling * jnp.einsum(
        "thd,the->hde", query_rows, grad_attn, preferred_element_type=jnp.float32
    )
    suffix_half = prefix_swapped(local_grads, True)
    grad_scores = (
        jnp.einsum("the,uhe->htu", grad_attn, value_rows, preferred_element_type=jnp.float32)
        * causal_mask
    ).astype(jnp.bfloat16)
    grad_query = scaling * (
        jnp.einsum("htu,uhd->thd", grad_scores, key_rows, preferred_element_type=jnp.float32)
        + jnp.einsum("the,hde->thd", grad_attn, prefix_half, preferred_element_type=jnp.float32)
    )
    grad_key = scaling * jnp.einsum(
        "htu,thd->uhd", grad_scores, query_rows, preferred_element_type=jnp.float32
    ) + jnp.einsum("uhe,hde->uhd", value_rows, suffix_half, preferred_element_type=jnp.float32)
    grad_value = jnp.einsum(
        "htu,the->uhe", scores, grad_attn, preferred_element_type=jnp.float32
    ) + jnp.einsum("uhd,hde->uhe", key_rows, suffix_half, preferred_element_type=jnp.float32)
    out_shape = (1, row_count, feature_count)
    return (
        output,
        grad_query.reshape(out_shape).astype(jnp.bfloat16),
        grad_key.reshape(out_shape).astype(jnp.bfloat16),
        grad_value.reshape(out_shape).astype(jnp.bfloat16),
        gain_grad,
    )


def solution(mesh):
    return jax.shard_map(
        per_device,
        mesh=mesh,
        in_specs=(
            P("dp", "seq", None),
            P("dp", "seq", None),
            P("dp", "seq", None),
            P(),
            P("dp", "seq", None),
        ),
        out_specs=(
            P("dp", "seq", None),
            P("dp", "seq", None),
            P("dp", "seq", None),
            P("dp", "seq", None),
            P(),
        ),
        check_vma=False,
    )
```

profile of v0, /device:TPU:1, one launch (start us, length us, event | category | flops | bytes accessed | tf_op | source)
XLA Modules:
  0.0 252.3 jit_solution(6267400844076144092)
XLA Ops:
  0.6 1.1 copy.128
  1.8 0.0 copy-start.13
  1.8 0.5 copy.92
  2.3 0.0 copy-start.3
  2.3 0.6 copy-done.13
  2.8 0.1 copy.129
  2.9 0.1 copy-done.3
  3.1 0.3 fusion.26
  3.4 38.4 %all_to_all.58 = f32[1,32,8192]{2,0,1:T(1,128)S(1)} all-to-all(f32[1,32,8192]{2,0,1:T(1,128)S(1)} %bitcast.94), channel_id=1, replica_groups=mesh['dp'=16,'seq'=32] {'seq'}, dimensions={1} | all-to-all | bytes 2097152 | tf_op jit(solution)/shard_map/all_to_all | solution.py:13
  41.7 1.3 fusion
  43.0 0.5 broadcast.107
  43.5 1.0 reduce.3
  44.6 1.2 reshape.208
  45.7 8.5 %all-to-all-start.1 = ((bf16[32,2,4096]{2,1,0:T(2,128)(2,1)}), bf16[32,2,4096]{2,1,0:T(2,128)(2,1)S(1)}, u32[]{:S(2)}, u32[]{:S(2)}) async-start(bf16[32,2,4096]{2,1,0:T(2,128)(2,1)} %reshape.208), calls=%async_computation.1 | async-start | bytes 1048576 | tf_op jit(solution)/shard_map/all_to_all | solution.py:21
  54.2 0.0 copy-start.9
  54.2 0.1 copy.127
  54.3 0.9 copy-done.9
  55.3 1.2 copy.99
  56.5 0.5 fusion.10
  57.0 1.5 convolution_bitcast_fusion.3
  58.5 9.7 %all-to-all-done.1 = bf16[32,2,4096]{2,1,0:T(2,128)(2,1)S(1)} async-done(((bf16[32,2,4096]{2,1,0:T(2,128)(2,1)}), bf16[32,2,4096]{2,1,0:T(2,128)(2,1)S(1)}, u32[]{:S(2)}, u32[]{:S(2)}) %all-to-all-start.1) | async-done | bytes 524320 | tf_op jit(solution)/shard_map/all_to_all | solution.py:21
  68.2 0.5 reshape.209
  68.7 4.0 %reduce.1 = bf16[32,8192]{1,0:T(8,128)(2,1)} reduce(bf16[32,1,8192]{2,1,0:T(2,128)(2,1)S(1)} %reshape.209, bf16[]{:T(256)} %constant.19), dimensions={1}, to_apply=%all_to_all.48.reduce_sub_computation | reduce | bytes 1048578 | tf_op jit(solution)/shard_map/all_to_all | solution.py:21
  72.7 1.3 reshape.200
  74.0 0.0 copy-start
  74.0 1.9 multiply_reduce_fusion
  75.9 0.0 copy-start.10
  75.9 0.0 copy-start.15
  75.9 1.4 copy.100
  77.3 1.7 fusion.20
  79.0 0.3 divide_convert_fusion
  79.4 1.3 fusion.3
  80.7 2.5 %copy.108 = f32[16,128,128]{2,1,0:T(8,128)} copy(f32[16,128,128]{1,2,0:T(8,128)} %fusion.3) | data formatting | bytes 2097152 | tf_op jit(solution)/shard_map/mul | solution.py:61
  83.2 8.1 %all-to-all-start.2 = ((f32[1,32,8192]{2,0,1:T(1,128)}), f32[1,32,8192]{2,0,1:T(1,128)}, u32[]{:S(2)}, u32[]{:S(2)}) async-start(f32[1,32,8192]{2,0,1:T(1,128)} %bitcast.93), calls=%async_computation.2 | async-start | bytes 2097152 | tf_op jit(solution)/shard_map/all_to_all | solution.py:13
  91.3 0.0 copy-start.4
  91.3 0.5 fusion.11
  91.9 0.5 copy-done.4
  92.4 0.5 convolution_bitcast_fusion.2
  92.9 0.3 copy-done.2
  93.2 0.4 copy-done.1
  93.6 1.1 fusion.9
  94.7 21.5 %all-to-all-done.2 = f32[1,32,8192]{2,0,1:T(1,128)} async-done(((f32[1,32,8192]{2,0,1:T(1,128)}), f32[1,32,8192]{2,0,1:T(1,128)}, u32[]{:S(2)}, u32[]{:S(2)}) %all-to-all-start.2) | async-done | bytes 1048608 | tf_op jit(solution)/shard_map/all_to_all | solution.py:13
  116.2 3.2 %fusion.1 = bf16[32,1,8192]{2,0,1:T(8,128)(2,1)} fusion(f32[1,32,8192]{2,0,1:T(1,128)} %all-to-all-done.2), kind=kOutput, calls=%fused_computation.3 | convolution fusion | flops 100926464 | bytes 1572864 | tf_op jit(solution)/shard_map/dot_general | solution.py:19
  119.4 2.7 %reduce.4 = bf16[32,8192]{1,0:T(8,128)(2,1)} reduce(bf16[32,1,8192]{2,0,1:T(8,128)(2,1)} %fusion.1, bf16[]{:T(256)} %broadcast.107), dimensions={1}, to_apply=%copy.110.reduce_sub_computation | reduce | bytes 1048578 | tf_op jit(solution)/shard_map/all_to_all | solution.py:21
  122.1 2.2 reshape.210
  124.3 8.3 %all-to-all-start.3 = ((bf16[32,2,4096]{2,1,0:T(2,128)(2,1)}), bf16[32,2,4096]{2,1,0:T(2,128)(2,1)}, u32[]{:S(2)}, u32[]{:S(2)}) async-start(bf16[32,2,4096]{2,1,0:T(2,128)(2,1)} %reshape.210), calls=%async_computation.3 | async-start | bytes 1048576 | tf_op jit(solution)/shard_map/all_to_all | solution.py:21
  132.6 2.4 fusion.4
  135.0 1.4 copy.98
  136.3 1.0 copy.116
  137.4 99.2 %psum.7 = f32[2048]{0:T(1024)S(1)} all-reduce(f32[2048]{0:T(1024)S(1)} %get-tuple-element.25), channel_id=1, replica_groups=mesh['dp'=16,'seq'=32] {'dp','seq'}, use_global_device_ids=true, to_apply=%region_3.0 | all-reduce | flops 2048 | bytes 16384 | tf_op jit(solution)/shard_map/psum | solution.py:52
  236.5 0.6 broadcast_multiply_fusion
  237.2 0.3 fusion.34
  237.4 0.9 copy-done.7
  238.4 1.0 multiply_convert_fusion
  239.4 0.0 all-to-all-done.3
  239.4 3.6 %reshape.211 = bf16[32,1,8192]{2,1,0:T(2,128)(2,1)S(1)} reshape(bf16[32,2,4096]{2,1,0:T(2,128)(2,1)} %all-to-all-done.3) | data formatting | bytes 1048576
  243.0 4.0 %reduce.2 = bf16[32,8192]{1,0:T(8,128)(2,1)} reduce(bf16[32,1,8192]{2,1,0:T(2,128)(2,1)S(1)} %reshape.211, bf16[]{:T(256)} %constant.19), dimensions={1}, to_apply=%all_to_all.53.reduce_sub_computation | reduce | bytes 1048578 | tf_op jit(solution)/shard_map/all_to_all | solution.py:21
  246.9 1.3 reshape.203
  248.2 0.5 fusion.13
  248.8 0.7 copy-done.6
  249.5 0.5 fusion.12
  249.9 0.3 copy.113
  250.2 1.0 copy.117
  251.2 1.0 copy.118
  (21 shorter events, 0.1 us)
Async XLA Ops:
  1.8 1.0 copy-start.13
  2.3 0.8 copy-start.3
  45.7 8.5 %copy-start.14 = (bf16[1,128,2048]{2,1,0:T(8,128)(2,1)S(1)}, bf16[1,128,2048]{2,1,0:T(8,128)(2,1)}, u32[]{:S(2)}) copy-start(bf16[1,128,2048]{2,1,0:T(8,128)(2,1)} %param.5) | copy-start | bytes 1572868
  45.7 22.5 %all-to-all-start.1 = ((bf16[32,2,4096]{2,1,0:T(2,128)(2,1)}), bf16[32,2,4096]{2,1,0:T(2,128)(2,1)S(1)}, u32[]{:S(2)}, u32[]{:S(2)}) async-start(bf16[32,2,4096]{2,1,0:T(2,128)(2,1)} %reshape.208), calls=%async_computation.1 | async-start | bytes 1048576 | tf_op jit(solution)/shard_map/all_to_all | solution.py:21
  54.2 1.0 copy-start.9
  57.0 1.6 copy-start.11
  74.0 1.9 copy-start
  75.9 1.4 copy-start.10
  75.9 1.4 copy-start.15
  77.3 1.7 copy-start.5
  83.2 32.9 %all-to-all-start.2 = ((f32[1,32,8192]{2,0,1:T(1,128)}), f32[1,32,8192]{2,0,1:T(1,128)}, u32[]{:S(2)}, u32[]{:S(2)}) async-start(f32[1,32,8192]{2,0,1:T(1,128)} %bitcast.93), calls=%async_computation.2 | async-start | bytes 2097152 | tf_op jit(solution)/shard_map/all_to_all | solution.py:13
  91.3 1.0 copy-start.4
  92.4 0.8 copy-start.2
  92.4 1.2 copy-start.1
  124.3 115.0 %all-to-all-start.3 = ((bf16[32,2,4096]{2,1,0:T(2,128)(2,1)}), bf16[32,2,4096]{2,1,0:T(2,128)(2,1)}, u32[]{:S(2)}, u32[]{:S(2)}) async-start(bf16[32,2,4096]{2,1,0:T(2,128)(2,1)} %reshape.210), calls=%async_computation.3 | async-start | bytes 1048576 | tf_op jit(solution)/shard_map/all_to_all | solution.py:21
  135.0 1.4 copy-start.8
  136.3 100.8 %copy-start.12 = (bf16[16,128,128]{2,1,0:T(8,128)(2,1)S(1)}, bf16[16,128,128]{2,1,0:T(8,128)(2,1)}, u32[]{:S(2)}) copy-start(bf16[16,128,128]{2,1,0:T(8,128)(2,1)} %copy-done.11) | copy-start | bytes 1572868
  237.2 1.2 copy-start.7
  248.2 1.2 copy-start.6
where the time goes:
time: 254 us; the launch traced here: 252 us
  blocking collectives  138 us (54%)
  waiting for transfers between devices  31.1 us (12%)
  local copies, waits for them, and re-layouts  26.8 us (11%)
  starting transfers between devices  24.8 us (10%)
  matrix products  15.8 us (6%)
  other arithmetic  15.3 us (6%)
    psum x1, blocking collectives, per_device(): total_gain = lax.psum(partial_gain, ('dp', 'seq'))  99.2 us
    all_to_all x1, blocking collectives, prefix_swapped(): lax.all_to_all(flat_state, 'seq', split_axis=1, concat_axis=0, tiled=True)  38.4 us
    all_to_all x1, waiting for transfers between devices, prefix_swapped(): lax.all_to_all(flat_state, 'seq', split_axis=1, concat_axis=0, tiled=True)  21.5 us
    all_to_all x2, starting transfers between devices, prefix_swapped(): lax.all_to_all(summed_half, 'seq', split_axis=0, concat_axis=1, tiled=True)  16.7 us
    unnamed x42, local copies, waits for them, and re-layouts  16.5 us
    all_to_all x4, other arithmetic, prefix_swapped(): lax.all_to_all(summed_half, 'seq', split_axis=0, concat_axis=1, tiled=True)  11.6 us
    all_to_all x2, waiting for transfers between devices, prefix_swapped(): lax.all_to_all(summed_half, 'seq', split_axis=0, concat_axis=1, tiled=True)  9.67 us
    all_to_all x1, starting transfers between devices, prefix_swapped(): lax.all_to_all(flat_state, 'seq', split_axis=1, concat_axis=0, tiled=True)  8.06 us
  transfers between devices with their start and end apart: 3, of which 2 were waited for; matrix products, arithmetic and copies ran while one was open for 5% of the time, Pallas kernels for 0%

commit v1 on v0

--- a/solution.py
+++ b/solution.py
@@ -49,7 +49,7 @@
     output = (gain * normalized).astype(jnp.bfloat16)[None]
     upstream = cotangent[0].astype(jnp.float32)
     partial_gain = jnp.sum(upstream * normalized, axis=0)
-    total_gain = lax.psum(partial_gain, ("dp", "seq"))
+    total_gain = jnp.sum(lax.all_gather(partial_gain, ("dp", "seq")), axis=0)
     gain_grad = total_gain / lax.axis_size("dp")
     scaled = upstream * gain
     inner_mean = jnp.mean(scaled * normalized, axis=-1, keepdims=True)

time: 254 us -> 225 us (0.89)
  blocking collectives: 138 us -> 38.4 us
  waiting for transfers between devices: 31.1 us -> 79 us
  between operations: 0.88 us -> 14.2 us
  local copies, waits for them, and re-layouts: 26.8 us -> 30.9 us
  other arithmetic: 15.3 us -> 19 us
    psum x1 -> x0, blocking collectives: 99.2 us -> none  [per_device(): total_gain = lax.psum(partial_gain, ('dp', 'seq'))]
    all_gather x0 -> x1, waiting for transfers between devices: none -> 39.1 us  [per_device(): total_gain = jnp.sum(lax.all_gather(partial_gain, ('dp', 'seq')), axis=0)]
    all_to_all x2, waiting for transfers between devices: 9.67 us -> 20.6 us  [prefix_swapped(): lax.all_to_all(summed_half, 'seq', split_axis=0, concat_axis=1, tiled=True)]
    all_gather x0 -> x1, local copies, waits for them, and re-layouts: none -> 4.91 us  [per_device(): total_gain = jnp.sum(lax.all_gather(partial_gain, ('dp', 'seq')), axis=0)]
    unnamed x42 -> x20, local copies, waits for them, and re-layouts: 16.5 us -> 15.6 us
  transfers between devices with their start and end apart: 3 -> 4, of which waited for: 2 -> 4; matrix products, arithmetic and copies ran while one was open for 5% -> 18% of each run, Pallas kernels for 0% -> 0%
where the time goes in v1:
time: 225 us; the launch traced here: 224 us
  waiting for transfers between devices  79 us (35%)
  blocking collectives  38.4 us (17%)
  local copies, waits for them, and re-layouts  30.9 us (14%)
  starting transfers between devices  24.7 us (11%)
  other arithmetic  19 us (8%)
  matrix products  17.5 us (8%)
  between operations  14.2 us (6%)
    all_gather x1, waiting for transfers between devices, per_device(): total_gain = jnp.sum(lax.all_gather(partial_gain, ('dp', 'seq')), axis=0)  39.1 us
    all_to_all x1, blocking collectives, prefix_swapped(): lax.all_to_all(flat_state, 'seq', split_axis=1, concat_axis=0, tiled=True)  38.4 us
    all_to_all x2, waiting for transfers between devices, prefix_swapped(): lax.all_to_all(summed_half, 'seq', split_axis=0, concat_axis=1, tiled=True)  20.6 us
    all_to_all x1, waiting for transfers between devices, prefix_swapped(): lax.all_to_all(flat_state, 'seq', split_axis=1, concat_axis=0, tiled=True)  19.2 us
    all_to_all x2, starting transfers between devices, prefix_swapped(): lax.all_to_all(summed_half, 'seq', split_axis=0, concat_axis=1, tiled=True)  16.7 us
    unnamed x20, local copies, waits for them, and re-layouts  15.6 us
    all_to_all x4, other arithmetic, prefix_swapped(): lax.all_to_all(summed_half, 'seq', split_axis=0, concat_axis=1, tiled=True)  11 us
    all_to_all x1, starting transfers between devices, prefix_swapped(): lax.all_to_all(flat_state, 'seq', split_axis=1, concat_axis=0, tiled=True)  8.01 us
  transfers between devices with their start and end apart: 4, of which 4 were waited for; matrix products, arithmetic and copies ran while one was open for 18% of the time, Pallas kernels for 0%

profile of v1, /device:TPU:1, one launch (start us, length us, event | category | flops | bytes accessed | tf_op | source)
XLA Modules:
  0.0 223.6 jit_solution(3601339159602107984)
XLA Ops:
  7.2 1.1 copy.158
  8.3 1.1 copy.159
  9.5 0.5 copy.122
  9.9 0.0 copy-start.1
  10.0 0.3 fusion.26
  10.3 38.4 %all_to_all.58 = f32[1,32,8192]{2,0,1:T(1,128)S(1)} all-to-all(f32[1,32,8192]{2,0,1:T(1,128)S(1)} %bitcast.94), channel_id=1, replica_groups=mesh['dp'=16,'seq'=32] {'seq'}, dimensions={1} | all-to-all | bytes 2097152 | tf_op jit(solution)/shard_map/all_to_all | solution.py:13
  48.6 1.3 fusion
  49.9 0.6 broadcast.107
  50.5 1.1 reduce.3
  51.6 1.2 reshape.209
  52.7 0.0 copy-done.1
  52.7 8.4 %all-to-all-start.1 = ((bf16[32,2,4096]{2,1,0:T(2,128)(2,1)}), bf16[32,2,4096]{2,1,0:T(2,128)(2,1)S(1)}, u32[]{:S(2)}, u32[]{:S(2)}) async-start(bf16[32,2,4096]{2,1,0:T(2,128)(2,1)} %reshape.209), calls=%async_computation.1 | async-start | bytes 1048576 | tf_op jit(solution)/shard_map/all_to_all | solution.py:21
  61.1 0.0 all-gather.3.cloned.1.call-start
  61.1 1.1 copy.157
  62.3 0.5 fusion.10
  62.8 0.0 copy-start.3
  62.8 0.8 copy-done.3
  63.6 1.5 convolution_bitcast_fusion.3
  65.1 10.0 %all-to-all-done.1 = bf16[32,2,4096]{2,1,0:T(2,128)(2,1)S(1)} async-done(((bf16[32,2,4096]{2,1,0:T(2,128)(2,1)}), bf16[32,2,4096]{2,1,0:T(2,128)(2,1)S(1)}, u32[]{:S(2)}, u32[]{:S(2)}) %all-to-all-start.1) | async-done | bytes 524320 | tf_op jit(solution)/shard_map/all_to_all | solution.py:21
  75.1 0.5 reshape.210
  75.6 0.0 copy-start.4
  75.6 4.0 %reduce.1 = bf16[32,8192]{1,0:T(8,128)(2,1)} reduce(bf16[32,1,8192]{2,1,0:T(2,128)(2,1)S(1)} %reshape.210, bf16[]{:T(256)} %constant.19), dimensions={1}, to_apply=%all_to_all.48.reduce_sub_computation | reduce | bytes 1048578 | tf_op jit(solution)/shard_map/all_to_all | solution.py:21
  79.6 1.3 reshape.200
  80.9 0.0 copy-start
  80.9 1.9 multiply_reduce_fusion
  82.8 1.3 copy.130
  84.1 0.0 copy-done.4
  84.1 2.4 %fusion.20 = (f32[2048]{0:T(1024)}, f32[128]{0:T(128)S(1)}) fusion(bf16[1,128,2048]{2,1,0:T(8,128)(2,1)} %param.9, f32[128,2048]{1,0:T(8,128)} %copy.130, f32[128]{0:T(128)S(1)} %add_sqrt_fusion, f32[2048]{0:T(1024)S(1)} %copy-done.4), kind=kLoop, calls=%fused_computation.34 | loop fusion | flops 1832832 | bytes 1590272 | tf_op jit(solution)/shard_map/reduce_sum | solution.py:51
  86.5 0.0 all-gather.3.cloned.1.call-update
  86.5 2.2 copy.129
  88.7 0.0 copy-done
  88.8 1.6 divide_convert_fusion
  90.3 1.3 fusion.3
  91.6 2.6 %copy.138 = f32[16,128,128]{2,1,0:T(8,128)} copy(f32[16,128,128]{1,2,0:T(8,128)} %fusion.3) | data formatting | bytes 2097152 | tf_op jit(solution)/shard_map/mul | solution.py:61
  94.2 8.0 %all-to-all-start.2 = ((f32[1,32,8192]{2,0,1:T(1,128)}), f32[1,32,8192]{2,0,1:T(1,128)}, u32[]{:S(2)}, u32[]{:S(2)}) async-start(f32[1,32,8192]{2,0,1:T(1,128)} %bitcast.93), calls=%async_computation.2 | async-start | bytes 2097152 | tf_op jit(solution)/shard_map/all_to_all | solution.py:13
  102.2 1.3 copy.128
  103.5 0.5 fusion.11
  104.0 1.5 convolution_bitcast_fusion.2
  105.6 1.3 fusion.9
  106.9 1.0 copy.146
  107.9 19.2 %all-to-all-done.2 = f32[1,32,8192]{2,0,1:T(1,128)} async-done(((f32[1,32,8192]{2,0,1:T(1,128)}), f32[1,32,8192]{2,0,1:T(1,128)}, u32[]{:S(2)}, u32[]{:S(2)}) %all-to-all-start.2) | async-done | bytes 1048608 | tf_op jit(solution)/shard_map/all_to_all | solution.py:13
  127.1 2.4 %fusion.1 = bf16[32,1,8192]{2,0,1:T(8,128)(2,1)S(1)} fusion(f32[1,32,8192]{2,0,1:T(1,128)} %all-to-all-done.2), kind=kOutput, calls=%fused_computation.3 | convolution fusion | flops 100926464 | bytes 1572864 | tf_op jit(solution)/shard_map/dot_general | solution.py:19
  129.6 1.7 reduce.4
  131.3 2.2 reshape.211
  133.5 8.3 %all-to-all-start.3 = ((bf16[32,2,4096]{2,1,0:T(2,128)(2,1)}), bf16[32,2,4096]{2,1,0:T(2,128)(2,1)}, u32[]{:S(2)}, u32[]{:S(2)}) async-start(bf16[32,2,4096]{2,1,0:T(2,128)(2,1)} %reshape.211), calls=%async_computation.3 | async-start | bytes 1048576 | tf_op jit(solution)/shard_map/all_to_all | solution.py:21
  141.9 0.0 copy-start.2
  141.9 1.4 fusion.4
  143.2 1.3 fusion.34
  144.6 0.0 copy-done.2
  144.6 1.0 multiply_convert_fusion
  145.6 10.7 %all-to-all-done.3 = bf16[32,2,4096]{2,1,0:T(2,128)(2,1)} async-done(((bf16[32,2,4096]{2,1,0:T(2,128)(2,1)}), bf16[32,2,4096]{2,1,0:T(2,128)(2,1)}, u32[]{:S(2)}, u32[]{:S(2)}) %all-to-all-start.3) | async-done | bytes 524320 | tf_op jit(solution)/shard_map/all_to_all | solution.py:21
  156.2 4.4 %reshape.212 = bf16[32,1,8192]{2,1,0:T(2,128)(2,1)} reshape(bf16[32,2,4096]{2,1,0:T(2,128)(2,1)} %all-to-all-done.3) | data formatting | bytes 1048576
  160.7 4.3 %reduce.2 = bf16[32,8192]{1,0:T(8,128)(2,1)S(1)} reduce(bf16[32,1,8192]{2,1,0:T(2,128)(2,1)} %reshape.212, bf16[]{:T(256)} %constant.19), dimensions={1}, to_apply=%all_to_all.53.reduce_sub_computation | reduce | bytes 1048578 | tf_op jit(solution)/shard_map/all_to_all | solution.py:21
  165.0 0.2 reshape.203
  165.2 1.7 fusion.12
  166.9 0.3 copy.143
  167.2 1.0 copy.147
  168.2 0.5 fusion.13
  168.8 1.0 copy.148
  169.8 39.1 %all-gather.3.cloned.1.call-done = f32[1048576]{0:T(1024)} async-done(((f32[2048]{0:T(1024)}), f32[1048576]{0:T(1024)}) %all-gather.3.cloned.1.call-update) | async-done | bytes 4194320 | tf_op jit(solution)/shard_map/all_gather | solution.py:52
  208.9 4.9 %reshape.206 = f32[512,2048]{1,0:T(8,128)} reshape(f32[1048576]{0:T(1024)} %all-gather.3.cloned.1.call-done) | data formatting | bytes 8388608 | tf_op jit(solution)/shard_map/all_gather | solution.py:52
  213.8 2.4 %reduce_sum.39 = f32[2048]{0:T(1024)S(1)} reduce(f32[512,2048]{1,0:T(8,128)} %reshape.206, f32[]{:T(128)} %constant.4.clone.1), dimensions={0}, to_apply=%region_3.0 | reduce | flops 1046528 | bytes 4202500 | tf_op jit(solution)/shard_map/reduce_sum | solution.py:52
  216.2 0.6 broadcast_multiply_fusion
  (4 shorter events, 0.0 us)
Async XLA Ops:
  9.9 42.8 %copy-start.1 = (bf16[128,16,128]{0,2,1:T(8,128)(2,1)}, bf16[128,16,128]{0,2,1:T(8,128)(2,1)S(1)}, u32[]{:S(2)}) copy-start(bf16[128,16,128]{0,2,1:T(8,128)(2,1)S(1)} %copy.122) | copy-start | bytes 1572868
  52.7 22.3 %all-to-all-start.1 = ((bf16[32,2,4096]{2,1,0:T(2,128)(2,1)}), bf16[32,2,4096]{2,1,0:T(2,128)(2,1)S(1)}, u32[]{:S(2)}, u32[]{:S(2)}) async-start(bf16[32,2,4096]{2,1,0:T(2,128)(2,1)} %reshape.209), calls=%async_computation.1 | async-start | bytes 1048576 | tf_op jit(solution)/shard_map/all_to_all | solution.py:21
  61.1 147.8 %all-gather.3.cloned.1.call-start = ((), (), s32[]{:S(2)}) async-start(), calls=%async_computation.4 | async-start | bytes 4202496 | tf_op jit(solution)/shard_map/all_gather | solution.py:52
  62.8 0.8 copy-start.3
  75.6 8.5 %copy-start.4 = (f32[2048]{0:T(1024)S(1)}, f32[2048]{0:T(1024)}, u32[]{:S(2)}) copy-start(f32[2048]{0:T(1024)} %param.8) | copy-start | bytes 24580
  80.9 7.9 %copy-start = (bf16[16,128,128]{2,1,0:T(8,128)(2,1)}, bf16[16,128,128]{2,1,0:T(8,128)(2,1)S(1)}, u32[]{:S(2)}) copy-start(bf16[16,128,128]{2,1,0:T(8,128)(2,1)S(1)} %reshape.200) | copy-start | bytes 1572868
  94.2 33.0 %all-to-all-start.2 = ((f32[1,32,8192]{2,0,1:T(1,128)}), f32[1,32,8192]{2,0,1:T(1,128)}, u32[]{:S(2)}, u32[]{:S(2)}) async-start(f32[1,32,8192]{2,0,1:T(1,128)} %bitcast.93), calls=%async_computation.2 | async-start | bytes 2097152 | tf_op jit(solution)/shard_map/all_to_all | solution.py:13
  133.5 22.7 %all-to-all-start.3 = ((bf16[32,2,4096]{2,1,0:T(2,128)(2,1)}), bf16[32,2,4096]{2,1,0:T(2,128)(2,1)}, u32[]{:S(2)}, u32[]{:S(2)}) async-start(bf16[32,2,4096]{2,1,0:T(2,128)(2,1)} %reshape.211), calls=%async_computation.3 | async-start | bytes 1048576 | tf_op jit(solution)/shard_map/all_to_all | solution.py:21
  141.9 2.7 %copy-start.2 = (f32[1,128,2048]{2,1,0:T(8,128)S(1)}, f32[1,128,2048]{2,1,0:T(8,128)}, u32[]{:S(2)}) copy-start(f32[1,128,2048]{2,1,0:T(8,128)} %copy.128) | copy-start | bytes 3145732
Sparse Core Ops, SparseCore 0:
  86.6 122.1 all-gather.2
